TPU v7x, 32 devices: a whole 2x2x4 slice. The times are simulated.
32 devices in a mesh: section: 4 (over y, core), seq: 8 (over z, x).
Axes of the slice: x: 2, y: 2, z: 4, core: 2. Of those that a mesh axis runs over, the one named last changes fastest.
Arguments:
- context: bfloat16 [2048, 8192], P('seq'), may hold values from -24 to 24, as said below
- memory: bfloat16 [512, 8192], P('seq'), may hold values from -24 to 24, as said below
- query_weight: bfloat16 [8192, 4096], P(None, 'section'), may hold values from -0.0625 to 0.0625
- key_weight: bfloat16 [8192, 512], P('seq', 'section'), may hold values from -0.0625 to 0.0625
- value_weight: bfloat16 [8192, 512], P('seq', 'section'), may hold values from -0.0625 to 0.0625
- query_down_map: bfloat16 [8192, 128], replicated, may hold values from -0.0625 to 0.0625
- query_up_map: bfloat16 [128, 4096], P(None, 'section'), may hold values from -0.5 to 0.5
- value_down_map: bfloat16 [8192, 128], P('seq'), may hold values from -0.0625 to 0.0625
- value_up_map: bfloat16 [128, 512], P(None, 'section'), may hold values from -0.5 to 0.5
- output_weight: bfloat16 [4096, 8192], P('section', 'seq'), may hold values from -1 to 1
- decoder_gain: float32 [8192], P('seq'), may hold values from 0.25 to 1.75
- document_slots: int32 [8], replicated, may hold values from 1 to 320, 512 in all
- normed_gradient: bfloat16 [512, 8192], P('section', 'seq'), may hold values from -6 to 6
Outputs:
- normed: bfloat16 [512, 8192], P('section', 'seq')
- grad_qa: float32 [8192, 128], P(('section', 'seq'))
- grad_va: float32 [8192, 128], P(('section', 'seq'))
- query_up_gradient: float32 [128, 4096], P(None, 'section')
- value_up_gradient: float32 [128, 512], P(None, 'section')
Inputs may be any that keep to these rules, and one draw needn't show every extreme that they name: `context`: values of the normed inputs lie in this range. `memory`: values of the normed inputs lie in this range. Documents lie end to end in order; document d has document_slots[d] memory slots and 4 document_slots[d] context tokens; the counts sum to 512.
All inputs are finite; a program needn't handle non-finite values.
Results may differ from a plain program's by a relative error of at most 0.014.
The roundings to bfloat16 on the way count: a program that leaves them out, or rounds other values in their place, can miss the bound.
Values may be sent and summed in bfloat16 or wider, within the bound.
No kernel may reach another device: no remote copies, remote signals or barrier semaphores. Data moves between devices by JAX's collectives and lax.ppermute only.
A program may use at most 192 MiB of HBM per device.

v0:
```python
import jax
import jax.numpy as jnp
from jax import lax
from jax.sharding import PartitionSpec as P

MODEL_DIM = 8192
adapter_scale = 0.25
epsilon = 1e-05
mask_fill = -1e30


def doc_index(units, doc_ends):
    return jnp.sum((units[:, None] >= doc_ends[None, :]).astype(jnp.int32), axis=1)


def leading_contract(left, right):
    return lax.dot_general(
        left, right, (((0,), (0,)), ((), ())), preferred_element_type=jnp.float32
    )


def trailing_contract(left, right):
    return lax.dot_general(
        left, right, (((1,), (1,)), ((), ())), preferred_element_type=jnp.float32
    )


def body(
    context,
    memory,
    query_weight,
    key_weight,
    value_weight,
    query_down_map,
    query_up_map,
    value_down_map,
    value_up_map,
    output_weight,
    decoder_gain,
    document_slots,
    normed_gradient,
):
    tok_dev = context.shape[0]
    slot_dev = memory.shape[0]
    keys_dev = tok_dev + slot_dev
    seq_size = lax.axis_size("seq")
    seq_index = lax.axis_index("seq")
    section_extent = lax.axis_size("section")
    head_dim = key_weight.shape[1]
    group_heads = query_weight.shape[1] // head_dim
    every_row = jnp.concatenate([context, memory], axis=0)
    key_portion = lax.all_gather(key_weight, "seq", axis=0, tiled=True)
    value_fragment = lax.all_gather(value_weight, "seq", axis=0, tiled=True)
    adapter_portion = lax.all_gather(value_down_map, "seq", axis=0, tiled=True)
    combined_rows = jnp.concatenate([key_portion, value_fragment, adapter_portion], axis=1)
    projected = jnp.dot(every_row, combined_rows, preferred_element_type=jnp.float32)
    query_reduced = jnp.dot(memory, query_down_map, preferred_element_type=jnp.float32).astype(
        jnp.bfloat16
    )
    value_reduced = projected[:, 2 * head_dim :].astype(jnp.bfloat16)
    query_rows_out = (
        jnp.dot(memory, query_weight, preferred_element_type=jnp.float32)
        + adapter_scale * jnp.dot(query_reduced, query_up_map, preferred_element_type=jnp.float32)
    ).astype(jnp.bfloat16)
    keys_local = projected[:, :head_dim].astype(jnp.bfloat16)
    values_local = (
        projected[:, head_dim : 2 * head_dim]
        + adapter_scale * jnp.dot(value_reduced, value_up_map, preferred_element_type=jnp.float32)
    ).astype(jnp.bfloat16)
    keys_all, value_rows_all = (
        lax.all_gather(keys_local, "seq", axis=0, tiled=True),
        lax.all_gather(values_local, "seq", axis=0, tiled=True),
    )
    key_rank = jnp.arange(seq_size * keys_dev, dtype=jnp.int32)
    key_owner = key_rank // keys_dev
    owner_valid = jnp.ones(key_rank.shape, dtype=bool)
    doc_ends = jnp.cumsum(document_slots)
    offset = key_rank % keys_dev
    is_context = offset < tok_dev
    key_unit = jnp.where(
        is_context, (key_owner * tok_dev + offset) // 4, key_owner * slot_dev + offset - tok_dev
    )
    key_doc = doc_index(key_unit, doc_ends)
    slot_unit = seq_index * slot_dev + jnp.arange(slot_dev, dtype=jnp.int32)
    row_unit = jnp.repeat(slot_unit, group_heads)
    row_doc = doc_index(row_unit, doc_ends)
    allowed = (
        (key_doc[None, :] == row_doc[:, None])
        & (is_context[None, :] | (key_unit[None, :] <= row_unit[:, None]))
        & owner_valid[None, :]
    )
    score_scale = head_dim ** (-0.5)
    query_rows = query_rows_out.reshape(slot_dev * group_heads, head_dim)
    scores = jnp.where(allowed, trailing_contract(query_rows, keys_all) * score_scale, mask_fill)
    row_top = jnp.max(scores, axis=1, keepdims=True)
    exponent = jnp.exp(scores - row_top)
    probability = exponent / jnp.sum(exponent, axis=1, keepdims=True)
    prob_low = probability.astype(jnp.bfloat16)
    attended = (
        jnp.dot(prob_low, value_rows_all, preferred_element_type=jnp.float32)
        .reshape(slot_dev, group_heads * head_dim)
        .astype(jnp.bfloat16)
    )
    slots_all = lax.all_gather(attended, "seq", axis=0, tiled=True)
    hidden = lax.psum_scatter(
        jnp.dot(slots_all, output_weight, preferred_element_type=jnp.float32),
        "section",
        scatter_dimension=0,
        tiled=True,
    )
    total_slots = slot_dev * seq_size
    weighted = total_slots ** (-0.5) * normed_gradient.astype(jnp.float32) * decoder_gain[None, :]
    square_sum, cross_sum = lax.psum(
        (jnp.sum(hidden * hidden, axis=1), jnp.sum(weighted * hidden, axis=1)), "seq"
    )
    inv_rms = lax.rsqrt(square_sum / MODEL_DIM + epsilon)
    normed = (hidden * inv_rms[:, None] * decoder_gain[None, :]).astype(jnp.bfloat16)
    d_hidden = (
        inv_rms[:, None] * weighted - hidden * (inv_rms**3 * cross_sum / MODEL_DIM)[:, None]
    ).astype(jnp.bfloat16)
    grads_all = lax.all_gather(d_hidden, "section", axis=0, tiled=True)
    d_attended = lax.psum_scatter(
        trailing_contract(grads_all, output_weight), "seq", scatter_dimension=0, tiled=True
    ).astype(jnp.bfloat16)
    grad_rows_local = d_attended.reshape(slot_dev * group_heads, head_dim)
    d_probs = trailing_contract(grad_rows_local, value_rows_all)
    center = jnp.sum(probability * d_probs, axis=1, keepdims=True)
    d_scores = (probability * (d_probs - center)).astype(jnp.bfloat16)
    query_gradient = (
        (score_scale * jnp.dot(d_scores, keys_all, preferred_element_type=jnp.float32))
        .reshape(slot_dev, group_heads * head_dim)
        .astype(jnp.bfloat16)
    )
    value_gradient = lax.psum_scatter(
        leading_contract(prob_low, grad_rows_local), "seq", scatter_dimension=0, tiled=True
    ).astype(jnp.bfloat16)
    query_up_portion = adapter_scale * leading_contract(query_reduced, query_gradient)
    value_up_portion = adapter_scale * leading_contract(value_reduced, value_gradient)
    query_up_gradient, value_up_gradient = lax.psum((query_up_portion, value_up_portion), "seq")
    query_portion = adapter_scale * trailing_contract(query_gradient, query_up_map)
    value_portion = adapter_scale * trailing_contract(value_gradient, value_up_map)
    query_backward, value_backward = lax.psum((query_portion, value_portion), "section")
    query_backward = query_backward.astype(jnp.bfloat16)
    value_backward = value_backward.astype(jnp.bfloat16)
    model_width = memory.shape[1]
    section_columns = model_width // section_extent
    section_index = lax.axis_index("section")
    memory_cols = lax.dynamic_slice_in_dim(
        memory, section_index * section_columns, section_columns, 1
    )
    row_cols = lax.dynamic_slice_in_dim(
        every_row, section_index * section_columns, section_columns, 1
    )
    grad_qa, grad_va = (
        lax.psum_scatter(
            leading_contract(memory_cols, query_backward), "seq", scatter_dimension=0, tiled=True
        ),
        lax.psum_scatter(
            leading_contract(row_cols, value_backward), "seq", scatter_dimension=0, tiled=True
        ),
    )
    return (normed, grad_qa, grad_va, query_up_gradient, value_up_gradient)


def solution(mesh):
    in_specs = (
        P("seq", None),
        P("seq", None),
        P(None, "section"),
        P("seq", "section"),
        P("seq", "section"),
        P(),
        P(None, "section"),
        P("seq", None),
        P(None, "section"),
        P("section", "seq"),
        P("seq"),
        P(),
        P("section", "seq"),
    )
    out_specs = (
        P("section", "seq"),
        P(("section", "seq"), None),
        P(("section", "seq"), None),
        P(None, "section"),
        P(None, "section"),
    )
    return jax.shard_map(body, mesh=mesh, in_specs=in_specs, out_specs=out_specs, check_vma=False)
```

profile of v0, /device:TPU:0, one launch (start us, length us, event | category | flops | bytes accessed | tf_op | source)
XLA Modules:
  0.0 713.7 jit_solution(12109832830738827667)
XLA Ops:
  9.5 2.4 convolution_convert_fusion
  13.2 8.8 %fusion.18 = bf16[64,1024]{1,0:T(8,128)(2,1)S(1)} fusion(f32[64,1024]{1,0:T(8,128)S(1)} %convolution_multiply_fusion.1, bf16[64,8192]{1,0:T(8,128)(2,1)S(1)} %copy-done.2, bf16[8192,1024]{1,0:T(8,128)(2,1)} %param.15), kind=kOutput, calls=%fused_computation.25 | convolution fusion | flops 1073872896 | bytes 18219008 | tf_op jit(solution)/shard_map/dot_general | solution.py:62
  22.5 4.7 constant_dynamic-update-slice_fusion.1
  28.2 33.8 %all-gather.6.cloned.1.call-done = bf16[8192,128]{1,0:T(8,128)(2,1)} async-done(((bf16[1024,128]{1,0:T(8,128)(2,1)}), bf16[8192,128]{1,0:T(8,128)(2,1)}) %all-gather.6.cloned.1.call-update) | async-done | bytes 2097168 | tf_op jit(solution)/shard_map/all_gather | solution.py:52
  62.0 49.8 %all-gather.8.cloned.1.call-done = bf16[8192,128]{1,0:T(8,128)(2,1)} async-done(((bf16[1024,128]{1,0:T(8,128)(2,1)}), bf16[8192,128]{1,0:T(8,128)(2,1)}) %all-gather.8.cloned.1.call-update) | async-done | bytes 2097168 | tf_op jit(solution)/shard_map/all_gather | solution.py:53
  111.8 49.8 %all-gather.10.cloned.1.call-done = bf16[8192,128]{1,0:T(8,128)(2,1)} async-done(((bf16[1024,128]{1,0:T(8,128)(2,1)}), bf16[8192,128]{1,0:T(8,128)(2,1)}) %all-gather.10.cloned.1.call-update) | async-done | bytes 2097168 | tf_op jit(solution)/shard_map/all_gather | solution.py:54
  161.6 7.2 %fusion.51 = (bf16[320,384]{1,0:T(8,128)(2,1)S(1)}, f32[320,384]{1,0:T(8,128)S(1)}) fusion(bf16[320,8192]{1,0:T(8,128)(2,1)} %constant_dynamic-update-slice_fusion, bf16[8192,128]{1,0:T(8,128)(2,1)} %all-gather.10.cloned.1.call-done, bf16[8192,128]{1,0:T(8,128)(2,1)} %all-gather.8.cloned.1.call-done, bf16[8192,128]{1,0:T(8,128)(2,1)} %all-gather.6.cloned.1.call-done), kind=kOutput, calls=%fused_computation.83 | convolution fusion | flops 2032263168 | bytes 12271616 | tf_op jit(solution)/shard_map/dot_general | solution.py:56
  168.8 32.0 %all_gather.24 = bf16[2560,128]{1,0:T(8,128)(2,1)S(1)} all-gather(bf16[320,128]{1,0:T(8,128)(2,1)S(1)} %slice.14), channel_id=1, replica_groups=mesh['section'=4,'seq'=8] {'seq'}, dimensions={0}, use_global_device_ids=true | all-gather | bytes 737280 | tf_op jit(solution)/shard_map/all_gather | solution.py:71
  201.0 32.0 %all_gather.25 = bf16[2560,128]{1,0:T(8,128)(2,1)S(1)} all-gather(bf16[320,128]{1,0:T(8,128)(2,1)S(1)} %fusion.23), channel_id=1, replica_groups=mesh['section'=4,'seq'=8] {'seq'}, dimensions={0}, use_global_device_ids=true | all-gather | bytes 737280 | tf_op jit(solution)/shard_map/all_gather | solution.py:72
  233.0 2.0 fusion.52
  235.9 1.3 fusion.6
  237.2 2.3 copy-done.1
  241.1 38.3 %all-gather.12.cloned.1.call-done = bf16[512,1024]{1,0:T(8,128)(2,1)} async-done(((bf16[64,1024]{1,0:T(8,128)(2,1)}), bf16[512,1024]{1,0:T(8,128)(2,1)}) %all-gather.12.cloned.1.call-update) | async-done | bytes 1048592 | tf_op jit(solution)/shard_map/all_gather | solution.py:104
  279.4 3.8 fusion.53
  283.5 29.8 %reduce-scatter.6.cloned.1.call-done = f32[128,1024]{1,0:T(8,128)} async-done(((f32[512,1024]{1,0:T(8,128)}), f32[128,1024]{1,0:T(8,128)}) %reduce-scatter.6.cloned.1.call-update) | async-done | bytes 524304 | tf_op jit(solution)/shard_map/reduce_scatter | solution.py:105
  314.5 21.4 %all-reduce = (f32[128]{0:T(128)S(1)}, f32[128]{0:T(128)S(1)}) all-reduce(f32[128]{0:T(128)S(1)} %get-tuple-element.6, f32[128]{0:T(128)S(1)} %get-tuple-element.5), channel_id=1, replica_groups=mesh['section'=4,'seq'=8] {'seq'}, use_global_device_ids=true, to_apply=%region_7.8 | all-reduce | flops 256 | bytes 2048 | tf_op jit(solution)/shard_map/psum | solution.py:113
  335.9 2.0 subtract_convert_fusion
  338.0 13.1 %all-gather.14.cloned.1.call-done = bf16[512,1024]{1,0:T(8,128)(2,1)} async-done(((bf16[128,1024]{1,0:T(8,128)(2,1)}), bf16[512,1024]{1,0:T(8,128)(2,1)}) %all-gather.14.cloned.1.call-update) | async-done | bytes 1048592 | tf_op jit(solution)/shard_map/all_gather | solution.py:121
  351.1 3.8 fusion.54
  355.0 68.5 %reduce-scatter.8.cloned.1.call-done = f32[64,1024]{1,0:T(8,128)} async-done(((f32[512,1024]{1,0:T(8,128)}), f32[64,1024]{1,0:T(8,128)}) %reduce-scatter.8.cloned.1.call-update) | async-done | bytes 262160 | tf_op jit(solution)/shard_map/reduce_scatter | solution.py:122
  424.6 4.4 fusion.12
  429.1 3.8 multiply_reduce_fusion
  435.6 57.8 %reduce-scatter.12.cloned.1.call-done = f32[320,128]{1,0:T(8,128)} async-done(((f32[2560,128]{1,0:T(8,128)}), f32[320,128]{1,0:T(8,128)}) %reduce-scatter.12.cloned.1.call-update) | async-done | bytes 163856 | tf_op jit(solution)/shard_map/reduce_scatter | solution.py:134
  493.4 1.8 convolution_multiply_fusion.4
  496.5 12.6 %all-reduce.7 = (bf16[64,128]{1,0:T(8,128)(2,1)S(1)}, bf16[320,128]{1,0:T(8,128)(2,1)S(1)}) all-reduce(f32[64,128]{1,0:T(8,128)S(1)} %convolution_multiply_fusion.5, f32[320,128]{1,0:T(8,128)S(1)} %convolution_multiply_fusion.2), channel_id=1, replica_groups=mesh['section'=4,'seq'=8] {'section'}, use_global_device_ids=true, to_apply=%region_12.13 | all-reduce | flops 49152 | bytes 294912 | tf_op jit(solution)/shard_map/psum | solution.py:142
  509.1 2.9 fusion.10
  512.1 2.3 fusion.24
  514.5 55.1 %all-reduce.6.cloned.1.call-done = (f32[128,1024]{1,0:T(8,128)}, f32[128,128]{1,0:T(8,128)}) async-done(((f32[128,1024]{1,0:T(8,128)}, f32[128,128]{1,0:T(8,128)}), (f32[128,1024]{1,0:T(8,128)}, f32[128,128]{1,0:T(8,128)})) %all-reduce.6.cloned.1.call-update) | async-done | bytes 589840 | tf_op jit(solution)/shard_map/psum | solution.py:139
  569.6 67.1 %reduce-scatter.14.cloned.1.call-done = f32[256,128]{1,0:T(8,128)} async-done(((f32[2048,128]{1,0:T(8,128)}), f32[256,128]{1,0:T(8,128)}) %reduce-scatter.14.cloned.1.call-update) | async-done | bytes 131088 | tf_op jit(solution)/shard_map/reduce_scatter | solution.py:158
  636.7 67.1 %reduce-scatter.10.cloned.1.call-done = f32[256,128]{1,0:T(8,128)} async-done(((f32[2048,128]{1,0:T(8,128)}), f32[256,128]{1,0:T(8,128)}) %reduce-scatter.10.cloned.1.call-update) | async-done | bytes 131088 | tf_op jit(solution)/shard_map/reduce_scatter | solution.py:155
  703.8 1.9 copy.25
  705.7 1.5 copy.26
  (76 shorter events, 14.5 us)
Async XLA Ops:
  7.2 272.2 %copy-start = (bf16[1024,1024]{1,0:T(8,128)(2,1)S(1)}, bf16[1024,1024]{1,0:T(8,128)(2,1)}, u32[]{:S(2)}) copy-start(bf16[1024,1024]{1,0:T(8,128)(2,1)} %param.22) | copy-start | bytes 6291460
  7.2 6.0 copy-start.2
  7.2 54.8 %all-gather.6.cloned.1.call-start = ((), (), s32[]{:S(2)}) async-start(), calls=%async_computation.5 | async-start | bytes 2359296 | tf_op jit(solution)/shard_map/all_gather | solution.py:52
  7.9 103.9 %all-gather.8.cloned.1.call-start = ((), (), s32[]{:S(2)}) async-start(), calls=%async_computation.6 | async-start | bytes 2359296 | tf_op jit(solution)/shard_map/all_gather | solution.py:53
  8.7 152.9 %all-gather.10.cloned.1.call-start = ((), (), s32[]{:S(2)}) async-start(), calls=%async_computation.7 | async-start | bytes 2359296 | tf_op jit(solution)/shard_map/all_gather | solution.py:54
  9.4 270.0 %all-gather.12.cloned.1.call-start = ((), (), s32[]{:S(2)}) async-start(), calls=%async_computation.8 | async-start | bytes 1179648 | tf_op jit(solution)/shard_map/all_gather | solution.py:104
  13.2 8.9 %copy-start.11 = (s32[8]{0:T(128)S(1)}, s32[8]{0:T(128)}, u32[]{:S(2)}) copy-start(s32[8]{0:T(128)} %param.24) | copy-start | bytes 100
  28.2 172.6 %copy-start.9 = (bf16[128,128]{1,0:T(8,128)(2,1)S(1)}, bf16[128,128]{1,0:T(8,128)(2,1)}, u32[]{:S(2)}) copy-start(bf16[128,128]{1,0:T(8,128)(2,1)} %param.21) | copy-start | bytes 98308
  168.8 66.3 %copy-start.8 = (bf16[320,384]{1,0:T(8,128)(2,1)}, bf16[320,384]{1,0:T(8,128)(2,1)S(1)}, u32[]{:S(2)}) copy-start(bf16[320,384]{1,0:T(8,128)(2,1)S(1)} %get-tuple-element.17) | copy-start | bytes 737284
  200.8 34.2 %copy-start.4 = (bf16[2560,128]{1,0:T(8,128)(2,1)}, bf16[2560,128]{1,0:T(8,128)(2,1)S(1)}, u32[]{:S(2)}) copy-start(bf16[2560,128]{1,0:T(8,128)(2,1)S(1)} %all_gather.24) | copy-start | bytes 1966084
  233.0 4.2 copy-start.3
  237.2 2.3 copy-start.1
  240.3 43.2 %copy-start.10 = (f32[1024]{0:T(1024)S(1)}, f32[1024]{0:T(1024)}, u32[]{:S(2)}) copy-start(f32[1024]{0:T(1024)} %param.23) | copy-start | bytes 12292
  240.3 73.0 %copy-start.7 = (bf16[128,1024]{1,0:T(8,128)(2,1)S(1)}, bf16[128,1024]{1,0:T(8,128)(2,1)}, u32[]{:S(2)}) copy-start(bf16[128,1024]{1,0:T(8,128)(2,1)} %param.25) | copy-start | bytes 786436
  241.1 72.2 %reduce-scatter.6.cloned.1.call-start = ((), (), s32[]{:S(2)}) async-start(), calls=%async_computation.9 | async-start | bytes 2621440 | tf_op jit(solution)/shard_map/reduce_scatter | solution.py:105
  283.2 67.9 %all-gather.14.cloned.1.call-start = ((), (), s32[]{:S(2)}) async-start(), calls=%async_computation.10 | async-start | bytes 1310720 | tf_op jit(solution)/shard_map/all_gather | solution.py:121
  337.9 85.6 %reduce-scatter.8.cloned.1.call-start = ((), (), s32[]{:S(2)}) async-start(), calls=%async_computation.11 | async-start | bytes 2359296 | tf_op jit(solution)/shard_map/reduce_scatter | solution.py:122
  355.0 138.4 %reduce-scatter.12.cloned.1.call-start = ((), (), s32[]{:S(2)}) async-start(), calls=%async_computation.13 | async-start | bytes 1474560 | tf_op jit(solution)/shard_map/reduce_scatter | solution.py:134
  429.0 3.9 slice-start
  429.0 140.6 %all-reduce.6.cloned.1.call-start = ((), (), s32[]{:S(2)}) async-start(), calls=%async_computation.15 | async-start | bytes 1179648 | tf_op jit(solution)/shard_map/psum | solution.py:139
  429.1 4.2 slice-start.1
  429.1 4.3 copy-start.5
  433.4 61.8 %copy-start.6 = (bf16[128,1024]{1,0:T(8,128)(2,1)S(1)}, bf16[128,1024]{1,0:T(8,128)(2,1)}, u32[]{:S(2)}) copy-start(bf16[128,1024]{1,0:T(8,128)(2,1)} %param.19) | copy-start | bytes 786436
  495.2 141.5 %reduce-scatter.14.cloned.1.call-start = ((), (), s32[]{:S(2)}) async-start(), calls=%async_computation.14 | async-start | bytes 1179648 | tf_op jit(solution)/shard_map/reduce_scatter | solution.py:158
  512.1 191.7 %reduce-scatter.10.cloned.1.call-start = ((), (), s32[]{:S(2)}) async-start(), calls=%async_computation.12 | async-start | bytes 1179648 | tf_op jit(solution)/shard_map/reduce_scatter | solution.py:155
Sparse Core Ops, SparseCore 0:
  10.1 51.8 all-gather.5
  64.1 47.6 all-gather.7
  113.9 47.6 all-gather.9
  241.2 38.1 all-gather.11
  283.4 29.8 reduce-scatter.5
  338.1 13.0 all-gather.13
  355.1 68.3 reduce-scatter.7
  429.1 64.1 reduce-scatter.11
  497.3 72.2 all-reduce.5
  573.4 63.2 reduce-scatter.13
  640.7 63.1 reduce-scatter.9
where the time goes:
time: 714 us
  waiting for transfers between devices  532 us (75%)
  blocking collectives  98 us (14%)
  matrix products  48.8 us (7%)
  between operations  14.2 us (2%)
  local copies, waits for them, and re-layouts  13 us (2%)
    reduce_scatter x1, waiting for transfers between devices, body(): lax.psum_scatter(trailing_contract(grads_all, output_weight), 'seq', scat...  68.5 us
    reduce_scatter x1, waiting for transfers between devices, body(): lax.psum_scatter(leading_contract(memory_cols, query_backward), 'seq', sc...  67.1 us
    reduce_scatter x1, waiting for transfers between devices, body(): lax.psum_scatter(leading_contract(row_cols, value_backward), 'seq', scatt...  67.1 us
    reduce_scatter x1, waiting for transfers between devices, body(): lax.psum_scatter(leading_contract(prob_low, grad_rows_local), 'seq', scat...  57.8 us
    psum x1, waiting for transfers between devices, body(): lax.psum((query_up_portion, value_up_portion), 'seq')  55.1 us
    all_gather x1, waiting for transfers between devices, body(): adapter_portion = lax.all_gather(value_down_map, 'seq', axis=0, tiled=True)  49.8 us
    all_gather x1, waiting for transfers between devices, body(): value_fragment = lax.all_gather(value_weight, 'seq', axis=0, tiled=True)  49.8 us
    all_gather x1, waiting for transfers between devices, body(): slots_all = lax.all_gather(attended, 'seq', axis=0, tiled=True)  38.3 us
  transfers between devices with their start and end apart: 11, of which 11 were waited for; matrix products, arithmetic and copies ran while one was open for 4% of the time, Pallas kernels for 0%

commit v1 on v0

--- a/solution.py
+++ b/solution.py
@@ -50,7 +50,12 @@
     group_heads = query_weight.shape[1] // head_dim
     every_row = jnp.concatenate([context, memory], axis=0)
     key_portion = lax.all_gather(key_weight, "seq", axis=0, tiled=True)
-    value_fragment = lax.all_gather(value_weight, "seq", axis=0, tiled=True)
+    ring = [value_weight]
+    for hop in range(7):
+        ring.append(lax.ppermute(ring[-1], "seq", [(dev, (dev + 1) % 8) for dev in range(8)]))
+    value_fragment = jnp.roll(
+        jnp.concatenate(ring[::-1], axis=0), (lax.axis_index("seq") + 1) * ring[0].shape[0], axis=0
+    )
     adapter_portion = lax.all_gather(value_down_map, "seq", axis=0, tiled=True)
     combined_rows = jnp.concatenate([key_portion, value_fragment, adapter_portion], axis=1)
     projected = jnp.dot(every_row, combined_rows, preferred_element_type=jnp.float32)

time: 714 us -> 681 us (0.954)
  waiting for transfers between devices: 532 us -> 480 us
  local copies, waits for them, and re-layouts: 13 us -> 26.1 us
    ppermute x0 -> x7, waiting for transfers between devices: none -> 67.9 us  [body(): lax.ppermute(ring[-1], 'seq', [(dev, (dev + 1) % 8) for dev in range(8)])]
    all_gather x1 -> x0, waiting for transfers between devices: 49.8 us -> none  [body(): value_fragment = lax.all_gather(value_weight, 'seq', axis=0, tiled=True)]
    all_gather x1, waiting for transfers between devices: 49.8 us -> 14.3 us  [body(): adapter_portion = lax.all_gather(value_down_map, 'seq', axis=0, tiled=True)]
    all_gather x1, waiting for transfers between devices: 33.8 us -> 0.02 us  [body(): key_portion = lax.all_gather(key_weight, 'seq', axis=0, tiled=True)]
    unnamed x31 -> x72, local copies, waits for them, and re-layouts: 10.9 us -> 20.3 us
  transfers between devices with their start and end apart: 11 -> 17, of which waited for: 11 -> 16; matrix products, arithmetic and copies ran while one was open for 4% -> 6% of each run, Pallas kernels for 0% -> 0%
where the time goes in v1:
time: 681 us; the launch traced here: 680 us
  waiting for transfers between devices  480 us (70%)
  blocking collectives  97.8 us (14%)
  matrix products  46.1 us (7%)
  local copies, waits for them, and re-layouts  26.1 us (4%)
  between operations  14.7 us (2%)
  other arithmetic  10.9 us (2%)
    reduce_scatter x1, waiting for transfers between devices, body(): lax.psum_scatter(trailing_contract(grads_all, output_weight), 'seq', scat...  68.5 us
    ppermute x7, waiting for transfers between devices, body(): lax.ppermute(ring[-1], 'seq', [(dev, (dev + 1) % 8) for dev in range(8)])  67.9 us
    reduce_scatter x1, waiting for transfers between devices, body(): lax.psum_scatter(leading_contract(row_cols, value_backward), 'seq', scatt...  67.2 us
    reduce_scatter x1, waiting for transfers between devices, body(): lax.psum_scatter(leading_contract(memory_cols, query_backward), 'seq', sc...  67 us
    reduce_scatter x1, waiting for transfers between devices, body(): lax.psum_scatter(leading_contract(prob_low, grad_rows_local), 'seq', scat...  57.7 us
    psum x1, waiting for transfers between devices, body(): lax.psum((query_up_portion, value_up_portion), 'seq')  55.2 us
    all_gather x1, waiting for transfers between devices, body(): slots_all = lax.all_gather(attended, 'seq', axis=0, tiled=True)  38.6 us
    all_gather x1, blocking collectives, body(): lax.all_gather(keys_local, 'seq', axis=0, tiled=True)  32 us
  transfers between devices with their start and end apart: 17, of which 16 were waited for; matrix products, arithmetic and copies ran while one was open for 6% of the time, Pallas kernels for 0%

profile of v1, /device:TPU:0, one launch (start us, length us, event | category | flops | bytes accessed | tf_op | source)
XLA Modules:
  0.0 679.5 jit_solution(7779054535208200079)
XLA Ops:
  8.0 3.0 collective-permute-start
  11.0 9.6 %collective-permute-done = bf16[1024,128]{1,0:T(8,128)(2,1)S(1)} collective-permute-done((bf16[1024,128]{1,0:T(8,128)(2,1)}, bf16[1024,128]{1,0:T(8,128)(2,1)S(1)}, u32[]{:S(2)}, u32[]{:S(2)}) %collective-permute-start) | collective-permute-done | bytes 262176 | tf_op jit(solution)/shard_map/ppermute | solution.py:55
  20.7 15.9 %collective-permute-done.1 = bf16[1024,128]{1,0:T(8,128)(2,1)} collective-permute-done((bf16[1024,128]{1,0:T(8,128)(2,1)S(1)}, bf16[1024,128]{1,0:T(8,128)(2,1)}, u32[]{:S(2)}, u32[]{:S(2)}) %collective-permute-start.1) | collective-permute-done | bytes 262176 | tf_op jit(solution)/shard_map/ppermute | solution.py:55
  36.5 2.5 constant_dynamic-update-slice_fusion.1
  39.0 6.8 %collective-permute-done.2 = bf16[1024,128]{1,0:T(8,128)(2,1)S(1)} collective-permute-done((bf16[1024,128]{1,0:T(8,128)(2,1)}, bf16[1024,128]{1,0:T(8,128)(2,1)S(1)}, u32[]{:S(2)}, u32[]{:S(2)}) %collective-permute-start.2) | collective-permute-done | bytes 262176 | tf_op jit(solution)/shard_map/ppermute | solution.py:55
  46.5 15.8 %collective-permute-done.3 = bf16[1024,128]{1,0:T(8,128)(2,1)S(1)} collective-permute-done((bf16[1024,128]{1,0:T(8,128)(2,1)S(1)}, bf16[1024,128]{1,0:T(8,128)(2,1)S(1)}, u32[]{:S(2)}, u32[]{:S(2)}) %collective-permute-start.3) | collective-permute-done | bytes 262176 | tf_op jit(solution)/shard_map/ppermute | solution.py:55
  62.3 9.0 %fusion.18 = bf16[64,1024]{1,0:T(8,128)(2,1)S(1)} fusion(f32[64,1024]{1,0:T(8,128)S(1)} %convolution_multiply_fusion.1, bf16[64,8192]{1,0:T(8,128)(2,1)S(1)} %copy-done.2, bf16[8192,1024]{1,0:T(8,128)(2,1)} %param.15), kind=kOutput, calls=%fused_computation.25 | convolution fusion | flops 1073872896 | bytes 18219008 | tf_op jit(solution)/shard_map/dot_general | solution.py:67
  71.3 6.3 collective-permute-done.4
  77.7 2.3 copy-done.4
  81.2 8.4 %collective-permute-done.5 = bf16[1024,128]{1,0:T(8,128)(2,1)} collective-permute-done((bf16[1024,128]{1,0:T(8,128)(2,1)}, bf16[1024,128]{1,0:T(8,128)(2,1)}, u32[]{:S(2)}, u32[]{:S(2)}) %collective-permute-start.5) | collective-permute-done | bytes 262176 | tf_op jit(solution)/shard_map/ppermute | solution.py:55
  96.5 5.2 collective-permute-done.6
  112.5 14.3 %all-gather.7.cloned.1.call-done = bf16[8192,128]{1,0:T(8,128)(2,1)} async-done(((bf16[1024,128]{1,0:T(8,128)(2,1)}), bf16[8192,128]{1,0:T(8,128)(2,1)}) %all-gather.7.cloned.1.call-update) | async-done | bytes 2097168 | tf_op jit(solution)/shard_map/all_gather | solution.py:59
  126.9 7.2 %fusion.50 = (bf16[320,384]{1,0:T(8,128)(2,1)S(1)}, f32[320,384]{1,0:T(8,128)S(1)}) fusion(bf16[320,8192]{1,0:T(8,128)(2,1)} %copy-done.4, bf16[8192,128]{1,0:T(8,128)(2,1)} %all-gather.7.cloned.1.call-done, bf16[8192,128]{1,0:T(8,128)(2,1)} %constant_dynamic-slice_fusion, bf16[8192,128]{1,0:T(8,128)(2,1)} %all-gather.5.cloned.1.call-done), kind=kOutput, calls=%fused_computation.100 | convolution fusion | flops 2032263168 | bytes 12271616 | tf_op jit(solution)/shard_map/dot_general | solution.py:61
  134.1 32.0 %all_gather.20 = bf16[2560,128]{1,0:T(8,128)(2,1)S(1)} all-gather(bf16[320,128]{1,0:T(8,128)(2,1)S(1)} %slice.14), channel_id=1, replica_groups=mesh['section'=4,'seq'=8] {'seq'}, dimensions={0}, use_global_device_ids=true | all-gather | bytes 737280 | tf_op jit(solution)/shard_map/all_gather | solution.py:76
  166.3 31.9 %all_gather.21 = bf16[2560,128]{1,0:T(8,128)(2,1)S(1)} all-gather(bf16[320,128]{1,0:T(8,128)(2,1)S(1)} %fusion.24), channel_id=1, replica_groups=mesh['section'=4,'seq'=8] {'seq'}, dimensions={0}, use_global_device_ids=true | all-gather | bytes 737280 | tf_op jit(solution)/shard_map/all_gather | solution.py:77
  202.3 2.4 copy-done.1
  206.3 38.6 %all-gather.9.cloned.1.call-done = bf16[512,1024]{1,0:T(8,128)(2,1)} async-done(((bf16[64,1024]{1,0:T(8,128)(2,1)}), bf16[512,1024]{1,0:T(8,128)(2,1)}) %all-gather.9.cloned.1.call-update) | async-done | bytes 1048592 | tf_op jit(solution)/shard_map/all_gather | solution.py:109
  244.9 3.8 fusion.52
  248.8 30.0 %reduce-scatter.6.cloned.1.call-done = f32[128,1024]{1,0:T(8,128)} async-done(((f32[512,1024]{1,0:T(8,128)}), f32[128,1024]{1,0:T(8,128)}) %reduce-scatter.6.cloned.1.call-update) | async-done | bytes 524304 | tf_op jit(solution)/shard_map/reduce_scatter | solution.py:110
  280.0 21.4 %all-reduce = (f32[128]{0:T(128)S(1)}, f32[128]{0:T(128)S(1)}) all-reduce(f32[128]{0:T(128)S(1)} %get-tuple-element.6, f32[128]{0:T(128)S(1)} %get-tuple-element.5), channel_id=1, replica_groups=mesh['section'=4,'seq'=8] {'seq'}, use_global_device_ids=true, to_apply=%region_7.8 | all-reduce | flops 256 | bytes 2048 | tf_op jit(solution)/shard_map/psum | solution.py:118
  303.5 13.1 %all-gather.11.cloned.1.call-done = bf16[512,1024]{1,0:T(8,128)(2,1)} async-done(((bf16[128,1024]{1,0:T(8,128)(2,1)}), bf16[512,1024]{1,0:T(8,128)(2,1)}) %all-gather.11.cloned.1.call-update) | async-done | bytes 1048592 | tf_op jit(solution)/shard_map/all_gather | solution.py:126
  316.6 3.9 fusion.53
  320.6 68.5 %reduce-scatter.8.cloned.1.call-done = f32[64,1024]{1,0:T(8,128)} async-done(((f32[512,1024]{1,0:T(8,128)}), f32[64,1024]{1,0:T(8,128)}) %reduce-scatter.8.cloned.1.call-update) | async-done | bytes 262160 | tf_op jit(solution)/shard_map/reduce_scatter | solution.py:127
  390.2 4.4 fusion.12
  394.7 3.8 multiply_reduce_fusion
  401.1 57.7 %reduce-scatter.12.cloned.1.call-done = f32[320,128]{1,0:T(8,128)} async-done(((f32[2560,128]{1,0:T(8,128)}), f32[320,128]{1,0:T(8,128)}) %reduce-scatter.12.cloned.1.call-update) | async-done | bytes 163856 | tf_op jit(solution)/shard_map/reduce_scatter | solution.py:139
  462.0 12.5 %all-reduce.7 = (bf16[64,128]{1,0:T(8,128)(2,1)S(1)}, bf16[320,128]{1,0:T(8,128)(2,1)S(1)}) all-reduce(f32[64,128]{1,0:T(8,128)S(1)} %convolution_multiply_fusion.5, f32[320,128]{1,0:T(8,128)S(1)} %convolution_multiply_fusion.2), channel_id=1, replica_groups=mesh['section'=4,'seq'=8] {'section'}, use_global_device_ids=true, to_apply=%region_12.13 | all-reduce | flops 49152 | bytes 294912 | tf_op jit(solution)/shard_map/psum | solution.py:147
  474.6 2.9 fusion.10
  477.6 2.3 fusion.22
  479.9 55.2 %all-reduce.6.cloned.1.call-done = (f32[128,1024]{1,0:T(8,128)}, f32[128,128]{1,0:T(8,128)}) async-done(((f32[128,1024]{1,0:T(8,128)}, f32[128,128]{1,0:T(8,128)}), (f32[128,1024]{1,0:T(8,128)}, f32[128,128]{1,0:T(8,128)})) %all-reduce.6.cloned.1.call-update) | async-done | bytes 589840 | tf_op jit(solution)/shard_map/psum | solution.py:144
  535.1 67.2 %reduce-scatter.14.cloned.1.call-done = f32[256,128]{1,0:T(8,128)} async-done(((f32[2048,128]{1,0:T(8,128)}), f32[256,128]{1,0:T(8,128)}) %reduce-scatter.14.cloned.1.call-update) | async-done | bytes 131088 | tf_op jit(solution)/shard_map/reduce_scatter | solution.py:163
  602.4 67.0 %reduce-scatter.10.cloned.1.call-done = f32[256,128]{1,0:T(8,128)} async-done(((f32[2048,128]{1,0:T(8,128)}), f32[256,128]{1,0:T(8,128)}) %reduce-scatter.10.cloned.1.call-update) | async-done | bytes 131088 | tf_op jit(solution)/shard_map/reduce_scatter | solution.py:160
  (130 shorter events, 40.1 us)
Async XLA Ops:
  7.2 237.7 %copy-start = (bf16[1024,1024]{1,0:T(8,128)(2,1)S(1)}, bf16[1024,1024]{1,0:T(8,128)(2,1)}, u32[]{:S(2)}) copy-start(bf16[1024,1024]{1,0:T(8,128)(2,1)} %param.22) | copy-start | bytes 6291460
  7.2 105.3 %all-gather.5.cloned.1.call-start = ((), (), s32[]{:S(2)}) async-start(), calls=%async_computation.5 | async-start | bytes 2359296 | tf_op jit(solution)/shard_map/all_gather | solution.py:52
  7.9 119.0 %all-gather.7.cloned.1.call-start = ((), (), s32[]{:S(2)}) async-start(), calls=%async_computation.6 | async-start | bytes 2359296 | tf_op jit(solution)/shard_map/all_gather | solution.py:59
  8.0 12.6 %collective-permute-start = (bf16[1024,128]{1,0:T(8,128)(2,1)}, bf16[1024,128]{1,0:T(8,128)(2,1)S(1)}, u32[]{:S(2)}, u32[]{:S(2)}) collective-permute-start(bf16[1024,128]{1,0:T(8,128)(2,1)} %param.17), channel_id=1, source_target_pairs={{0,1},{1,2},{2,3},{3,4},{4,5},{5,6},{6,7},{7,0},{8,9},{9,10},{10,1... | collective-permute-start | bytes 786440 | tf_op jit(solution)/shard_map/ppermute | solution.py:55
  20.5 16.0 %collective-permute-start.1 = (bf16[1024,128]{1,0:T(8,128)(2,1)S(1)}, bf16[1024,128]{1,0:T(8,128)(2,1)}, u32[]{:S(2)}, u32[]{:S(2)}) collective-permute-start(bf16[1024,128]{1,0:T(8,128)(2,1)S(1)} %collective-permute-done), channel_id=1, source_target_pairs={{0,1},{1,2},{2,3},{3,4},{4,5},{5,6},{6,7},{7,0},{8,9},{9,10},{10,1... | collective-permute-start | bytes 786440 | tf_op jit(solution)/shard_map/ppermute | solution.py:55
  20.6 224.3 %all-gather.9.cloned.1.call-start = ((), (), s32[]{:S(2)}) async-start(), calls=%async_computation.7 | async-start | bytes 1179648 | tf_op jit(solution)/shard_map/all_gather | solution.py:109
  36.5 9.3 %collective-permute-start.2 = (bf16[1024,128]{1,0:T(8,128)(2,1)}, bf16[1024,128]{1,0:T(8,128)(2,1)S(1)}, u32[]{:S(2)}, u32[]{:S(2)}) collective-permute-start(bf16[1024,128]{1,0:T(8,128)(2,1)} %collective-permute-done.1), channel_id=1, source_target_pairs={{0,1},{1,2},{2,3},{3,4},{4,5},{5,6},{6,7},{7,0},{8,9},{9,10},{10,1... | collective-permute-start | bytes 786440 | tf_op jit(solution)/shard_map/ppermute | solution.py:55
  45.8 16.5 %collective-permute-start.3 = (bf16[1024,128]{1,0:T(8,128)(2,1)S(1)}, bf16[1024,128]{1,0:T(8,128)(2,1)S(1)}, u32[]{:S(2)}, u32[]{:S(2)}) collective-permute-start(bf16[1024,128]{1,0:T(8,128)(2,1)S(1)} %collective-permute-done.2), channel_id=1, source_target_pairs={{0,1},{1,2},{2,3},{3,4},{4,5},{5,6},{6,7},{7,0},{8,9},{9,10},{10,1... | collective-permute-start | bytes 786440 | tf_op jit(solution)/shard_map/ppermute | solution.py:55
  62.3 15.3 %collective-permute-start.4 = (bf16[1024,128]{1,0:T(8,128)(2,1)S(1)}, bf16[1024,128]{1,0:T(8,128)(2,1)}, u32[]{:S(2)}, u32[]{:S(2)}) collective-permute-start(bf16[1024,128]{1,0:T(8,128)(2,1)S(1)} %collective-permute-done.3), channel_id=1, source_target_pairs={{0,1},{1,2},{2,3},{3,4},{4,5},{5,6},{6,7},{7,0},{8,9},{9,10},{10,1... | collective-permute-start | bytes 786440 | tf_op jit(solution)/shard_map/ppermute | solution.py:55
  71.3 36.5 %copy-start.8 = (bf16[1024,128]{1,0:T(8,128)(2,1)S(1)}, bf16[1024,128]{1,0:T(8,128)(2,1)}, u32[]{:S(2)}) copy-start(bf16[1024,128]{1,0:T(8,128)(2,1)} %param.17) | copy-start | bytes 786436
  77.6 12.1 %collective-permute-start.5 = (bf16[1024,128]{1,0:T(8,128)(2,1)}, bf16[1024,128]{1,0:T(8,128)(2,1)}, u32[]{:S(2)}, u32[]{:S(2)}) collective-permute-start(bf16[1024,128]{1,0:T(8,128)(2,1)} %collective-permute-done.4), channel_id=1, source_target_pairs={{0,1},{1,2},{2,3},{3,4},{4,5},{5,6},{6,7},{7,0},{8,9},{9,10},{10,1... | collective-permute-start | bytes 786440 | tf_op jit(solution)/shard_map/ppermute | solution.py:55
  80.0 29.8 %copy-start.14 = (bf16[1024,128]{1,0:T(8,128)(2,1)S(1)}, bf16[1024,128]{1,0:T(8,128)(2,1)}, u32[]{:S(2)}) copy-start(bf16[1024,128]{1,0:T(8,128)(2,1)} %copy-done.13) | copy-start | bytes 786436
  80.0 29.9 %copy-start.12 = (bf16[1024,128]{1,0:T(8,128)(2,1)S(1)}, bf16[1024,128]{1,0:T(8,128)(2,1)}, u32[]{:S(2)}) copy-start(bf16[1024,128]{1,0:T(8,128)(2,1)} %copy-done.11) | copy-start | bytes 786436
  80.0 30.9 %copy-start.10 = (bf16[1024,128]{1,0:T(8,128)(2,1)S(1)}, bf16[1024,128]{1,0:T(8,128)(2,1)}, u32[]{:S(2)}) copy-start(bf16[1024,128]{1,0:T(8,128)(2,1)} %copy-done.9) | copy-start | bytes 786436
  89.7 12.1 %collective-permute-start.6 = (bf16[1024,128]{1,0:T(8,128)(2,1)}, bf16[1024,128]{1,0:T(8,128)(2,1)S(1)}, u32[]{:S(2)}, u32[]{:S(2)}) collective-permute-start(bf16[1024,128]{1,0:T(8,128)(2,1)} %collective-permute-done.5), channel_id=1, source_target_pairs={{0,1},{1,2},{2,3},{3,4},{4,5},{5,6},{6,7},{7,0},{8,9},{9,10},{10,1... | collective-permute-start | bytes 786440 | tf_op jit(solution)/shard_map/ppermute | solution.py:55
  112.5 53.6 %copy-start.20 = (bf16[128,128]{1,0:T(8,128)(2,1)S(1)}, bf16[128,128]{1,0:T(8,128)(2,1)}, u32[]{:S(2)}) copy-start(bf16[128,128]{1,0:T(8,128)(2,1)} %param.21) | copy-start | bytes 98308
  112.5 85.6 %copy-start.19 = (bf16[512,128]{1,0:T(8,128)(2,1)S(1)}, bf16[512,128]{1,0:T(8,128)(2,1)}, u32[]{:S(2)}) copy-start(bf16[512,128]{1,0:T(8,128)(2,1)} %reshape.136) | copy-start | bytes 393220
  112.5 85.6 %copy-start.21 = (s32[2560]{0:T(1024)S(1)}, s32[2560]{0:T(1024)}, u32[]{:S(2)}) copy-start(s32[2560]{0:T(1024)} %fusion.38) | copy-start | bytes 30724
  112.5 85.6 %copy-start.23 = (s32[512]{0:T(512)S(1)}, s32[512]{0:T(512)}, u32[]{:S(2)}) copy-start(s32[512]{0:T(512)} %ge.31) | copy-start | bytes 6148
  112.5 85.6 %copy-start.24 = (pred[2560]{0:T(1024)(128)(4,1)S(1)}, pred[2560]{0:T(1024)(128)(4,1)}, u32[]{:S(2)}) copy-start(pred[2560]{0:T(1024)(128)(4,1)} %fusion.41) | copy-start | bytes 7684
  134.1 66.1 %copy-start.18 = (bf16[320,384]{1,0:T(8,128)(2,1)}, bf16[320,384]{1,0:T(8,128)(2,1)S(1)}, u32[]{:S(2)}) copy-start(bf16[320,384]{1,0:T(8,128)(2,1)S(1)} %get-tuple-element.17) | copy-start | bytes 737284
  166.1 34.1 %copy-start.5 = (bf16[2560,128]{1,0:T(8,128)(2,1)}, bf16[2560,128]{1,0:T(8,128)(2,1)S(1)}, u32[]{:S(2)}) copy-start(bf16[2560,128]{1,0:T(8,128)(2,1)S(1)} %all_gather.20) | copy-start | bytes 1966084
  206.3 42.5 %copy-start.22 = (f32[1024]{0:T(1024)S(1)}, f32[1024]{0:T(1024)}, u32[]{:S(2)}) copy-start(f32[1024]{0:T(1024)} %param.23) | copy-start | bytes 12292
  206.3 72.5 %copy-start.17 = (bf16[128,1024]{1,0:T(8,128)(2,1)S(1)}, bf16[128,1024]{1,0:T(8,128)(2,1)}, u32[]{:S(2)}) copy-start(bf16[128,1024]{1,0:T(8,128)(2,1)} %param.25) | copy-start | bytes 786436
  206.3 72.5 %reduce-scatter.6.cloned.1.call-start = ((), (), s32[]{:S(2)}) async-start(), calls=%async_computation.8 | async-start | bytes 2621440 | tf_op jit(solution)/shard_map/reduce_scatter | solution.py:110
  248.8 67.9 %all-gather.11.cloned.1.call-start = ((), (), s32[]{:S(2)}) async-start(), calls=%async_computation.9 | async-start | bytes 1310720 | tf_op jit(solution)/shard_map/all_gather | solution.py:126
  303.5 85.6 %reduce-scatter.8.cloned.1.call-start = ((), (), s32[]{:S(2)}) async-start(), calls=%async_computation.10 | async-start | bytes 2359296 | tf_op jit(solution)/shard_map/reduce_scatter | solution.py:127
  320.5 138.3 %reduce-scatter.12.cloned.1.call-start = ((), (), s32[]{:S(2)}) async-start(), calls=%async_computation.12 | async-start | bytes 1474560 | tf_op jit(solution)/shard_map/reduce_scatter | solution.py:139
  394.6 140.5 %all-reduce.6.cloned.1.call-start = ((), (), s32[]{:S(2)}) async-start(), calls=%async_computation.14 | async-start | bytes 1179648 | tf_op jit(solution)/shard_map/psum | solution.py:144
  399.0 61.8 %copy-start.16 = (bf16[128,1024]{1,0:T(8,128)(2,1)S(1)}, bf16[128,1024]{1,0:T(8,128)(2,1)}, u32[]{:S(2)}) copy-start(bf16[128,1024]{1,0:T(8,128)(2,1)} %param.19) | copy-start | bytes 786436
  460.7 141.7 %reduce-scatter.14.cloned.1.call-start = ((), (), s32[]{:S(2)}) async-start(), calls=%async_computation.13 | async-start | bytes 1179648 | tf_op jit(solution)/shard_map/reduce_scatter | solution.py:163
  477.6 191.8 %reduce-scatter.10.cloned.1.call-start = ((), (), s32[]{:S(2)}) async-start(), calls=%async_computation.11 | async-start | bytes 1179648 | tf_op jit(solution)/shard_map/reduce_scatter | solution.py:160
  (12 other events, 150.3 us)
Sparse Core Ops, SparseCore 0:
  10.1 62.6 all-gather.4
  75.0 51.8 all-gather.6
  206.4 38.4 all-gather.8
  248.9 29.8 reduce-scatter.5
  303.6 13.0 all-gather.10
  320.6 68.4 reduce-scatter.7
  394.7 64.0 reduce-scatter.11
  462.8 72.2 all-reduce.5
  539.1 63.2 reduce-scatter.13
  606.2 63.1 reduce-scatter.9
